TPU v7x, 256 devices: a whole 4x4x8 slice. The times are simulated.
256 devices in a mesh: space: 32 (over z, x), sample: 8 (over y, core).
Axes of the slice: x: 4, y: 4, z: 8, core: 2. Of those that a mesh axis runs over, the one named last changes fastest.
Arguments:
- crops: bfloat16 [256, 16, 64, 1024], P('sample', None, 'space'), may hold values from -6 to 6
- first_kernel: bfloat16 [32, 16, 3, 3, 3], replicated, may hold values from -0.3125 to 0.3125
- second_kernel: bfloat16 [64, 32, 3, 3, 3], replicated, may hold values from -0.21875 to 0.21875
- out_grad: bfloat16 [256, 64, 16, 64], P(('sample', 'space')), may hold values from -0.03125 to 0.03125
Outputs:
- features_out: bfloat16 [256, 64, 16, 64], P(('sample', 'space'))
- first_grad: float32 [32, 16, 3, 3, 3], replicated
- second_grad: float32 [64, 32, 3, 3, 3], replicated
All inputs are finite; a program needn't handle non-finite values.
Results may differ from a plain program's by a relative error of at most 0.012.
Values may be sent and summed in bfloat16 or wider, within the bound.
A program may use at most 128 MiB of HBM per device.

v0:
```python
import jax
import jax.numpy as jnp
from jax import lax
from jax.sharding import PartitionSpec as P

HEIGHT = 8
WIDTH = 128


def forward_conv(field, kernel, depth_pad):
    return lax.conv_general_dilated(
        field,
        kernel,
        (2, 2, 2),
        (depth_pad, (1, 0), (1, 0)),
        dimension_numbers=("NCDHW", "OIDHW", "NCDHW"),
        preferred_element_type=jnp.float32,
    )


def kernel_grad(field, cotangent, depth_pad):
    return lax.conv_general_dilated(
        field,
        cotangent,
        (1, 1, 1),
        (depth_pad, (1, 0), (1, 0)),
        rhs_dilation=(2, 2, 2),
        dimension_numbers=("CNDHW", "IODHW", "CNDHW"),
        preferred_element_type=jnp.float32,
    )


def input_grad(cotangent, kernel):
    flipped = kernel[:, :, ::-1, ::-1, ::-1]
    return lax.conv_general_dilated(
        cotangent,
        flipped,
        (1, 1, 1),
        ((1, 2), (1, 2), (1, 2)),
        lhs_dilation=(2, 2, 2),
        dimension_numbers=("NCDHW", "IODHW", "NCDHW"),
        preferred_element_type=jnp.float32,
    )


def silu_slope(value):
    sigma = jax.nn.sigmoid(value)
    return sigma * (1.0 + value * (1.0 - sigma))


def body(crops, first_kernel, second_kernel, out_grad):
    local_samples, channels_in, planes, flat_cells = crops.shape
    whole_input = lax.all_to_all(crops, "space", split_axis=0, concat_axis=2, tiled=True)
    whole_input = whole_input.reshape(
        whole_input.shape[0], channels_in, whole_input.shape[2], HEIGHT, WIDTH
    )
    first_pre = forward_conv(whole_input, first_kernel, (1, 0))
    act_whole = jax.nn.silu(first_pre).astype(jnp.bfloat16)
    sample_count = act_whole.shape[0]
    second_pre = forward_conv(act_whole, second_kernel, (1, 0))
    features_out = second_pre.astype(jnp.bfloat16).reshape(out_grad.shape)
    cotangent = out_grad.reshape(
        sample_count, out_grad.shape[1], out_grad.shape[2], HEIGHT // 4, WIDTH // 4
    )
    second_grad = kernel_grad(act_whole, cotangent, (1, 0))
    act_grad = input_grad(cotangent, second_kernel).astype(jnp.bfloat16)
    pre_grad = (act_grad.astype(jnp.float32) * silu_slope(first_pre)).astype(jnp.bfloat16)
    first_grad = kernel_grad(whole_input, pre_grad, (1, 0))
    flat = jnp.concatenate([first_grad.reshape(-1), second_grad.reshape(-1)])
    flat = lax.psum(flat, ("space", "sample"))
    first_grad = flat[: first_grad.size].reshape(first_grad.shape)
    second_grad = flat[first_grad.size :].reshape(second_grad.shape)
    return (features_out, first_grad, second_grad)


def solution(mesh):
    placed = (P("sample", None, "space", None), P(), P(), P(("sample", "space"), None, None, None))
    return jax.shard_map(
        body,
        mesh=mesh,
        in_specs=placed,
        out_specs=(P(("sample", "space"), None, None, None), P(), P()),
        check_vma=False,
    )
```

profile of v0, /device:TPU:1, one launch (start us, length us, event | category | flops | bytes accessed | tf_op | source)
XLA Modules:
  0.0 600.1 jit_solution(7680147417381081335)
XLA Ops:
  7.2 0.0 copy-start
  7.2 0.0 copy-start.3
  7.2 12.0 %all-to-all-start = ((bf16[32,16,2,1024]{3,2,1,0:T(2,128)(2,1)}), bf16[32,16,2,1024]{3,2,1,0:T(2,128)(2,1)S(1)}, u32[]{:S(2)}, u32[]{:S(2)}) async-start(bf16[32,16,2,1024]{3,2,1,0:T(2,128)(2,1)} %param.4), calls=%async_computation | async-start | bytes 4194304 | tf_op jit(solution)/shard_map/all_to_all | solution.py:53
  19.2 0.0 all-reduce.2.cloned.1.call-start
  19.3 1.2 copy.80
  20.5 0.2 copy.103
  20.7 0.1 pad.4.clone
  20.7 0.1 copy.83
  20.8 0.0 copy-done
  20.9 0.0 copy-done.3
  20.9 2.5 fusion.19
  23.3 5.4 copy.84
  28.7 38.9 %all-to-all-done = bf16[32,16,2,1024]{3,2,1,0:T(2,128)(2,1)S(1)} async-done(((bf16[32,16,2,1024]{3,2,1,0:T(2,128)(2,1)}), bf16[32,16,2,1024]{3,2,1,0:T(2,128)(2,1)S(1)}, u32[]{:S(2)}, u32[]{:S(2)}) %all-to-all-start) | async-done | bytes 2097184 | tf_op jit(solution)/shard_map/all_to_all | solution.py:53
  67.7 0.7 copy.68
  68.4 0.6 copy.104
  69.0 4.9 copy.102
  73.9 5.6 pad.clone
  79.5 0.0 copy-start.4
  79.5 0.0 copy-start.5
  79.5 32.4 %copy.71 = bf16[16,64,8,1,8,18]{0,4,5,2,1,3:T(8,128)(2,1)} copy(bf16[16,64,8,1,8,18]{1,2,5,4,0,3:T(8,128)(2,1)} %bitcast.50) | data formatting | bytes 4718592 | tf_op jit(solution)/shard_map/conv_general_dilated | solution.py:11
  111.9 3.9 slice.33
  115.8 0.0 copy-done.4
  115.8 0.0 copy-done.5
  115.8 20.2 %broadcast_select_fusion = (bf16[32,4,8,9,32]{4,2,3,1,0:T(8,128)(2,1)}, bf16[32,4,8,9,32]{4,2,3,1,0:T(8,128)(2,1)}, f32[32,4,8,9,32]{4,2,3,1,0:T(8,128)}) fusion(pred[8,9]{0,1:T(8,128)(4,1)S(1)} %copy-done.4, bf16[32,16,3,3,3]{0,1,4,3,2:T(8,128)(2,1)S(1)} %copy-done.5, bf16[16,64,8,1,7,2]{0,4,5,2,1,3:T(8,128)(2,1)} %slice.33, ...), kind=kOutput, calls=%fused_computation.30 | convolution fusion | flops 241065984 | bytes 4975688 | tf_op jit(solution)/shard_map/conv_general_dilated | solution.py:11
  136.0 2.6 copy.72
  138.6 0.0 copy-start.2
  138.6 0.4 slice.34
  139.1 1.4 copy.74
  140.4 0.0 copy-start.1
  140.4 1.0 fusion.48
  141.5 0.4 copy-done.1
  141.9 0.0 slice-start
  141.9 0.0 copy-done.2
  141.9 0.0 slice-start.1
  141.9 0.9 copy.89
  142.8 1.8 slice.40
  144.5 0.0 slice-done
  144.6 0.0 slice-done.1
  144.6 1.6 add_multiply_fusion
  146.2 4.8 copy.85
  151.0 11.8 %fusion.9 = f32[64,32,3,3,3]{0,1,4,3,2:T(8,128)S(1)} fusion(bf16[32,4,1,64,32]{4,0,3,1,2:T(8,128)(2,1)} %slice.40, bf16[1,64,16,2,32]{1,4,3,2,0:T(8,128)(2,1)S(1)} %bitcast.62), kind=kOutput, calls=%fused_computation.16 | convolution fusion | flops 91443200 | bytes 876544 | tf_op jit(solution)/shard_map/conv_general_dilated | solution.py:22
  162.9 12.3 %copy.93 = f32[64,32,3,3,3]{4,3,2,1,0:T(4,128)} copy(f32[64,32,3,3,3]{0,1,4,3,2:T(8,128)S(1)} %fusion.9) | data formatting | bytes 442368 | tf_op jit(solution)/shard_map/conv_general_dilated | solution.py:22
  175.2 11.0 %reshape.48 = f32[55296]{0:T(1024)} reshape(f32[64,32,3,3,3]{4,3,2,1,0:T(4,128)} %copy.93) | data formatting | bytes 442368 | tf_op jit(solution)/shard_map/reshape | solution.py:69
  186.1 34.9 %copy.86 = bf16[1,16,64,8,128]{1,0,4,3,2:T(2,128)(2,1)} copy(bf16[1,16,64,8,128]{4,3,1,2,0:T(8,128)(2,1)S(1)} %bitcast.49) | data formatting | bytes 4194304 | tf_op jit(solution)/shard_map/reshape | solution.py:54
  221.0 4.5 fusion.8
  225.5 89.8 %fusion.11 = f32[32,16,3,3,3]{0,1,4,3,2:T(8,128)} fusion(bf16[1,16,64,8,128]{1,0,4,3,2:T(2,128)(2,1)} %copy.86, bf16[32,4,1,64,32]{4,0,3,1,2:T(8,128)(2,1)S(1)} %fusion.8), kind=kOutput, calls=%fused_computation.18 | convolution fusion | flops 204385280 | bytes 2676736 | tf_op jit(solution)/shard_map/conv_general_dilated | solution.py:22
  315.3 4.4 copy.88
  319.7 2.0 reshape.47
  321.7 1.7 pad_maximum_fusion
  323.4 0.0 all-reduce.2.cloned.1.call-update
  323.4 3.5 fusion.26
  326.9 0.2 copy.77
  327.1 1.1 copy.94
  328.1 239.1 %all-reduce.2.cloned.1.call-done = f32[69120]{0:T(1024)} async-done(((f32[69120]{0:T(1024)}), f32[69120]{0:T(1024)}) %all-reduce.2.cloned.1.call-update) | async-done | bytes 276496 | tf_op jit(solution)/shard_map/psum | solution.py:70
  567.2 0.8 slice.41
  568.1 1.6 reshape.49
  569.6 2.5 copy.95
  572.1 1.0 slice.42
  573.1 8.3 %reshape.50 = f32[64,32,3,3,3]{4,3,2,1,0:T(4,128)} reshape(f32[55296]{0:T(1024)S(1)} %slice.42) | data formatting | bytes 442368 | tf_op jit(solution)/shard_map/reshape | solution.py:72
  581.4 11.7 %copy.96 = f32[64,32,3,3,3]{0,1,4,3,2:T(8,128)} copy(f32[64,32,3,3,3]{4,3,2,1,0:T(4,128)} %reshape.50) | data formatting | bytes 442368
  (2 shorter events, 0.0 us)
Async XLA Ops:
  7.2 13.7 %copy-start = (bf16[64,32,3,3,3]{0,1,4,3,2:T(8,128)(2,1)S(1)}, bf16[64,32,3,3,3]{0,1,4,3,2:T(8,128)(2,1)}, u32[]{:S(2)}) copy-start(bf16[64,32,3,3,3]{0,1,4,3,2:T(8,128)(2,1)} %param.6) | copy-start | bytes 331780
  7.2 13.7 %copy-start.3 = (pred[8,10]{0,1:T(8,128)(4,1)S(1)}, pred[8,10]{0,1:T(8,128)(4,1)}, u32[]{:S(2)}) copy-start(pred[8,10]{0,1:T(8,128)(4,1)} %constant.19) | copy-start | bytes 244
  7.2 60.5 %all-to-all-start = ((bf16[32,16,2,1024]{3,2,1,0:T(2,128)(2,1)}), bf16[32,16,2,1024]{3,2,1,0:T(2,128)(2,1)S(1)}, u32[]{:S(2)}, u32[]{:S(2)}) async-start(bf16[32,16,2,1024]{3,2,1,0:T(2,128)(2,1)} %param.4), calls=%async_computation | async-start | bytes 4194304 | tf_op jit(solution)/shard_map/all_to_all | solution.py:53
  19.2 548.0 %all-reduce.2.cloned.1.call-start = ((), (), s32[]{:S(2)}) async-start(), calls=%async_computation.1 | async-start | bytes 557056 | tf_op jit(solution)/shard_map/psum | solution.py:70
  79.5 36.3 %copy-start.4 = (pred[8,9]{0,1:T(8,128)(4,1)S(1)}, pred[8,9]{0,1:T(8,128)(4,1)}, u32[]{:S(2)}) copy-start(pred[8,9]{0,1:T(8,128)(4,1)} %constant.17) | copy-start | bytes 220
  79.5 36.3 %copy-start.5 = (bf16[32,16,3,3,3]{0,1,4,3,2:T(8,128)(2,1)S(1)}, bf16[32,16,3,3,3]{0,1,4,3,2:T(8,128)(2,1)}, u32[]{:S(2)}) copy-start(bf16[32,16,3,3,3]{0,1,4,3,2:T(8,128)(2,1)} %param.5) | copy-start | bytes 82948
  138.6 3.3 copy-start.2
  140.4 1.5 copy-start.1
  141.9 2.7 slice-start
  141.9 2.7 slice-start.1
Sparse Core Ops, SparseCore 0:
  323.5 243.6 all-reduce.1
where the time goes:
time: 607 us; the launch traced here: 600 us
  waiting for transfers between devices  278 us (46%)
  local copies, waits for them, and re-layouts  160 us (26%)
  matrix products  128 us (21%)
  between operations  14.4 us (2%)
  starting transfers between devices  12.1 us (2%)
  other arithmetic  7.78 us (1%)
    psum x1, waiting for transfers between devices, body(): flat = lax.psum(flat, ('space', 'sample'))  239 us
    conv_general_dilated x2, matrix products, kernel_grad(): lax.conv_general_dilated(field, cotangent, (1, 1, 1), (depth_pad, (1, 0),...  102 us
    reshape x2, local copies, waits for them, and re-layouts, body(): whole_input.reshape(whole_input.shape[0], channels_in, whole_input.shape[...  40.5 us
    all_to_all x1, waiting for transfers between devices, body(): lax.all_to_all(crops, 'space', split_axis=0, concat_axis=2, tiled=True)  38.9 us
    conv_general_dilated x2, local copies, waits for them, and re-layouts, forward_conv(): lax.conv_general_dilated(field, kernel, (2, 2, 2), (depth_pad, (1, 0), (1...  36.3 us
    conv_general_dilated x2, matrix products, forward_conv(): lax.conv_general_dilated(field, kernel, (2, 2, 2), (depth_pad, (1, 0), (1...  23.7 us
    unnamed x23, local copies, waits for them, and re-layouts  22.7 us
    conv_general_dilated x2, local copies, waits for them, and re-layouts, kernel_grad(): lax.conv_general_dilated(field, cotangent, (1, 1, 1), (depth_pad, (1, 0),...  16.7 us
  transfers between devices with their start and end apart: 2, of which 2 were waited for; matrix products, arithmetic and copies ran while one was open for 2% of the time, Pallas kernels for 0%

commit v1 on v0

--- a/solution.py
+++ b/solution.py
@@ -5,6 +5,7 @@
 
 HEIGHT = 8
 WIDTH = 128
+bind_rails_up = lambda xin: lax.psum(lax.psum(xin, "sample"), "space")
 
 
 def forward_conv(field, kernel, depth_pad):
@@ -67,7 +68,7 @@
     pre_grad = (act_grad.astype(jnp.float32) * silu_slope(first_pre)).astype(jnp.bfloat16)
     first_grad = kernel_grad(whole_input, pre_grad, (1, 0))
     flat = jnp.concatenate([first_grad.reshape(-1), second_grad.reshape(-1)])
-    flat = lax.psum(flat, ("space", "sample"))
+    flat = bind_rails_up(flat)
     first_grad = flat[: first_grad.size].reshape(first_grad.shape)
     second_grad = flat[first_grad.size :].reshape(second_grad.shape)
     return (features_out, first_grad, second_grad)

time: 607 us -> 574 us (0.946)
  waiting for transfers between devices: 278 us -> 240 us
    psum x1 -> x2, waiting for transfers between devices: 239 us -> 201 us  [bind_rails_up = lambda xin: lax.psum(lax.psum(xin, 'sample'), 'space')]
    unnamed x23 -> x21, local copies, waits for them, and re-layouts: 22.7 us -> 22.3 us
  transfers between devices with their start and end apart: 2 -> 3, of which waited for: 2 -> 3; matrix products, arithmetic and copies ran while one was open for 2% -> 3% of each run, Pallas kernels for 0% -> 0%
where the time goes in v1:
time: 574 us; the launch traced here: 564 us
  waiting for transfers between devices  240 us (42%)
  local copies, waits for them, and re-layouts  162 us (28%)
  matrix products  127 us (22%)
  between operations  14.5 us (3%)
  starting transfers between devices  12.1 us (2%)
  other arithmetic  7.78 us (1%)
    psum x2, waiting for transfers between devices, bind_rails_up = lambda xin: lax.psum(lax.psum(xin, 'sample'), 'space')  201 us
    conv_general_dilated x2, matrix products, kernel_grad(): lax.conv_general_dilated(field, cotangent, (1, 1, 1), (depth_pad, (1, 0),...  102 us
    reshape x2, local copies, waits for them, and re-layouts, body(): whole_input.reshape(whole_input.shape[0], channels_in, whole_input.shape[...  40.6 us
    all_to_all x1, waiting for transfers between devices, body(): lax.all_to_all(crops, 'space', split_axis=0, concat_axis=2, tiled=True)  38.9 us
    conv_general_dilated x2, local copies, waits for them, and re-layouts, forward_conv(): lax.conv_general_dilated(field, kernel, (2, 2, 2), (depth_pad, (1, 0), (1...  36.3 us
    conv_general_dilated x2, matrix products, forward_conv(): lax.conv_general_dilated(field, kernel, (2, 2, 2), (depth_pad, (1, 0), (1...  23.5 us
    unnamed x21, local copies, waits for them, and re-layouts  22.3 us
    conv_general_dilated x2, local copies, waits for them, and re-layouts, kernel_grad(): lax.conv_general_dilated(field, cotangent, (1, 1, 1), (depth_pad, (1, 0),...  16.8 us
  transfers between devices with their start and end apart: 3, of which 3 were waited for; matrix products, arithmetic and copies ran while one was open for 3% of the time, Pallas kernels for 0%

profile of v1, /device:TPU:1, one launch (start us, length us, event | category | flops | bytes accessed | tf_op | source)
XLA Modules:
  0.0 563.8 jit_solution(12953845877035143694)
XLA Ops:
  7.2 0.0 copy-start
  7.2 0.0 copy-start.2
  7.2 12.0 %all-to-all-start = ((bf16[32,16,2,1024]{3,2,1,0:T(2,128)(2,1)}), bf16[32,16,2,1024]{3,2,1,0:T(2,128)(2,1)S(1)}, u32[]{:S(2)}, u32[]{:S(2)}) async-start(bf16[32,16,2,1024]{3,2,1,0:T(2,128)(2,1)} %param.4), calls=%async_computation | async-start | bytes 4194304 | tf_op jit(solution)/shard_map/all_to_all | solution.py:54
  19.2 0.0 all-reduce.3.cloned.1.call-start
  19.3 1.2 copy.80
  20.5 0.2 copy.103
  20.7 0.1 pad.4.clone
  20.7 0.1 copy.83
  20.8 0.0 copy-done
  20.9 0.0 copy-done.2
  20.9 2.4 fusion.19
  23.3 5.4 copy.84
  28.7 38.9 %all-to-all-done = bf16[32,16,2,1024]{3,2,1,0:T(2,128)(2,1)S(1)} async-done(((bf16[32,16,2,1024]{3,2,1,0:T(2,128)(2,1)}), bf16[32,16,2,1024]{3,2,1,0:T(2,128)(2,1)S(1)}, u32[]{:S(2)}, u32[]{:S(2)}) %all-to-all-start) | async-done | bytes 2097184 | tf_op jit(solution)/shard_map/all_to_all | solution.py:54
  67.7 0.7 copy.68
  68.4 0.6 copy.104
  69.0 4.9 copy.102
  73.9 5.6 pad.clone
  79.5 0.0 copy-start.3
  79.6 0.0 copy-start.4
  79.6 32.5 %copy.71 = bf16[16,64,8,1,8,18]{0,4,5,2,1,3:T(8,128)(2,1)} copy(bf16[16,64,8,1,8,18]{1,2,5,4,0,3:T(8,128)(2,1)} %bitcast.50) | data formatting | bytes 4718592 | tf_op jit(solution)/shard_map/conv_general_dilated | solution.py:12
  112.0 3.9 slice.33
  115.9 0.0 copy-done.3
  115.9 0.0 copy-done.4
  115.9 20.2 %broadcast_select_fusion = (bf16[32,4,8,9,32]{4,2,3,1,0:T(8,128)(2,1)}, bf16[32,4,8,9,32]{4,2,3,1,0:T(8,128)(2,1)}, f32[32,4,8,9,32]{4,2,3,1,0:T(8,128)}) fusion(pred[8,9]{0,1:T(8,128)(4,1)S(1)} %copy-done.3, bf16[32,16,3,3,3]{0,1,4,3,2:T(8,128)(2,1)S(1)} %copy-done.4, bf16[16,64,8,1,7,2]{0,4,5,2,1,3:T(8,128)(2,1)} %slice.33, ...), kind=kOutput, calls=%fused_computation.30 | convolution fusion | flops 241065984 | bytes 4975688 | tf_op jit(solution)/shard_map/conv_general_dilated | solution.py:12
  136.1 2.6 copy.72
  138.6 0.0 copy-start.1
  138.7 0.4 slice.34
  139.1 2.6 copy.74
  141.7 0.0 slice-start
  141.7 0.0 copy-done.1
  141.7 0.0 slice-start.1
  141.8 0.9 copy.89
  142.7 1.8 slice.40
  144.4 0.0 slice-done
  144.4 0.0 slice-done.1
  144.4 1.6 add_multiply_fusion
  146.0 4.9 copy.85
  150.9 11.8 %fusion.9 = f32[64,32,3,3,3]{0,1,4,3,2:T(8,128)S(1)} fusion(bf16[32,4,1,64,32]{4,0,3,1,2:T(8,128)(2,1)} %slice.40, bf16[1,64,16,2,32]{1,4,3,2,0:T(8,128)(2,1)S(1)} %bitcast.62), kind=kOutput, calls=%fused_computation.16 | convolution fusion | flops 91443200 | bytes 876544 | tf_op jit(solution)/shard_map/conv_general_dilated | solution.py:23
  162.7 12.4 %copy.93 = f32[64,32,3,3,3]{4,3,2,1,0:T(4,128)} copy(f32[64,32,3,3,3]{0,1,4,3,2:T(8,128)S(1)} %fusion.9) | data formatting | bytes 442368 | tf_op jit(solution)/shard_map/conv_general_dilated | solution.py:23
  175.2 11.0 %reshape.48 = f32[55296]{0:T(1024)} reshape(f32[64,32,3,3,3]{4,3,2,1,0:T(4,128)} %copy.93) | data formatting | bytes 442368 | tf_op jit(solution)/shard_map/reshape | solution.py:70
  186.1 35.0 %copy.86 = bf16[1,16,64,8,128]{1,0,4,3,2:T(2,128)(2,1)} copy(bf16[1,16,64,8,128]{4,3,1,2,0:T(8,128)(2,1)S(1)} %bitcast.49) | data formatting | bytes 4194304 | tf_op jit(solution)/shard_map/reshape | solution.py:55
  221.1 4.5 fusion.8
  225.6 89.8 %fusion.11 = f32[32,16,3,3,3]{0,1,4,3,2:T(8,128)} fusion(bf16[1,16,64,8,128]{1,0,4,3,2:T(2,128)(2,1)} %copy.86, bf16[32,4,1,64,32]{4,0,3,1,2:T(8,128)(2,1)S(1)} %fusion.8), kind=kOutput, calls=%fused_computation.18 | convolution fusion | flops 204385280 | bytes 2676736 | tf_op jit(solution)/shard_map/conv_general_dilated | solution.py:23
  315.4 4.4 copy.88
  319.8 2.0 reshape.47
  321.8 1.7 pad_maximum_fusion
  323.4 0.0 all-reduce.3.cloned.1.call-update
  323.5 0.0 all-reduce.5.cloned.1.call-start
  323.5 1.1 fusion.48
  324.6 61.6 %all-reduce.3.cloned.1.call-done = f32[69120]{0:T(1024)} async-done(((f32[69120]{0:T(1024)}), f32[69120]{0:T(1024)}) %all-reduce.3.cloned.1.call-update) | async-done | bytes 276496 | tf_op jit(solution)/shard_map/psum | solution.py:8
  386.3 0.0 all-reduce.5.cloned.1.call-update
  386.3 3.3 fusion.26
  389.6 0.2 copy.77
  389.8 1.1 copy.94
  390.8 139.8 %all-reduce.5.cloned.1.call-done = f32[69120]{0:T(1024)} async-done(((f32[69120]{0:T(1024)}), f32[69120]{0:T(1024)}) %all-reduce.5.cloned.1.call-update) | async-done | bytes 276496 | tf_op jit(solution)/shard_map/psum | solution.py:8
  530.7 0.8 slice.41
  531.5 1.8 reshape.49
  533.3 2.5 copy.95
  535.8 1.0 slice.42
  536.7 8.3 %reshape.50 = f32[64,32,3,3,3]{4,3,2,1,0:T(4,128)} reshape(f32[55296]{0:T(1024)S(1)} %slice.42) | data formatting | bytes 442368 | tf_op jit(solution)/shard_map/reshape | solution.py:73
  545.1 11.7 %copy.96 = f32[64,32,3,3,3]{0,1,4,3,2:T(8,128)} copy(f32[64,32,3,3,3]{4,3,2,1,0:T(4,128)} %reshape.50) | data formatting | bytes 442368
  (2 shorter events, 0.0 us)
Async XLA Ops:
  7.2 13.7 %copy-start = (bf16[64,32,3,3,3]{0,1,4,3,2:T(8,128)(2,1)S(1)}, bf16[64,32,3,3,3]{0,1,4,3,2:T(8,128)(2,1)}, u32[]{:S(2)}) copy-start(bf16[64,32,3,3,3]{0,1,4,3,2:T(8,128)(2,1)} %param.6) | copy-start | bytes 331780
  7.2 13.7 %copy-start.2 = (pred[8,10]{0,1:T(8,128)(4,1)S(1)}, pred[8,10]{0,1:T(8,128)(4,1)}, u32[]{:S(2)}) copy-start(pred[8,10]{0,1:T(8,128)(4,1)} %constant.19) | copy-start | bytes 244
  7.2 60.5 %all-to-all-start = ((bf16[32,16,2,1024]{3,2,1,0:T(2,128)(2,1)}), bf16[32,16,2,1024]{3,2,1,0:T(2,128)(2,1)S(1)}, u32[]{:S(2)}, u32[]{:S(2)}) async-start(bf16[32,16,2,1024]{3,2,1,0:T(2,128)(2,1)} %param.4), calls=%async_computation | async-start | bytes 4194304 | tf_op jit(solution)/shard_map/all_to_all | solution.py:54
  19.2 367.1 %all-reduce.3.cloned.1.call-start = ((), (), s32[]{:S(2)}) async-start(), calls=%async_computation.1 | async-start | bytes 557056 | tf_op jit(solution)/shard_map/psum | solution.py:8
  79.5 36.3 %copy-start.3 = (pred[8,9]{0,1:T(8,128)(4,1)S(1)}, pred[8,9]{0,1:T(8,128)(4,1)}, u32[]{:S(2)}) copy-start(pred[8,9]{0,1:T(8,128)(4,1)} %constant.17) | copy-start | bytes 220
  79.6 36.3 %copy-start.4 = (bf16[32,16,3,3,3]{0,1,4,3,2:T(8,128)(2,1)S(1)}, bf16[32,16,3,3,3]{0,1,4,3,2:T(8,128)(2,1)}, u32[]{:S(2)}) copy-start(bf16[32,16,3,3,3]{0,1,4,3,2:T(8,128)(2,1)} %param.5) | copy-start | bytes 82948
  138.6 3.1 copy-start.1
  141.7 2.7 slice-start
  141.7 2.7 slice-start.1
  323.5 207.2 %all-reduce.5.cloned.1.call-start = ((), (), s32[]{:S(2)}) async-start(), calls=%async_computation.2 | async-start | bytes 557056 | tf_op jit(solution)/shard_map/psum | solution.py:8
Sparse Core Ops, SparseCore 0:
  323.6 62.6 all-reduce.2
  390.1 140.5 all-reduce.4
